TPU v7x, 32 devices: a whole 2x2x4 slice. The times are simulated.
32 devices in a mesh: parts: 2 (over y), space: 16 (over z, x, core).
Axes of the slice: x: 2, y: 2, z: 4, core: 2. Of those that a mesh axis runs over, the one named last changes fastest.
Arguments:
- snapshots: bfloat16 [2176, 8192], P('space', 'parts'), parts along dimension 1
- starts: int32 [16], replicated, may hold values from 0 to 1920, as said below
- bins: int32 [32], replicated, may hold values from 0 to 128
- mode_count: int32 [32], replicated, may hold values from 4 to 16
Outputs:
- modes: bfloat16 [32, 32, 8192], P(None, None, ('parts', 'space')), parts along dimension 2
- factor: float32 [64, 32, 32], P('parts'), parts along dimension 0
There are 2 independent parts, one for each index of `parts`. A program takes and returns all parts, laid end to end along the dimension named above; an argument that names none is the same for every part. Nothing has to cross between parts.
Inputs may be any that keep to these rules, and one draw needn't show every extreme that they name: Block starts rise; the first block starts at 0, the last at 1920, and successive starts differ by 64 to 192 snapshots.
All inputs are finite; a program needn't handle non-finite values.
Results may differ from a plain program's by a relative error of at most 0.008.
Values may be sent and summed in bfloat16 or wider, within the bound.
No kernel may reach another device: no remote copies, remote signals or barrier semaphores. Data moves between devices by JAX's collectives and lax.ppermute only.
A program may use at most 64 MiB of HBM per device.

v0:
```python
import math
import jax
import jax.numpy as jnp
from jax import lax
from jax.sharding import PartitionSpec as P

NB = 16
NWIN = 256
NFREQ = 32


def make_table(bins):
    offsets = jnp.arange(NWIN, dtype=jnp.int32)
    window = 0.5 - 0.5 * jnp.cos(2.0 * math.pi * offsets.astype(jnp.float32) / NWIN)
    scaling = 1.0 / jnp.sqrt(jnp.sum(window * window))
    turns = bins[:, None] * offsets[None, :] % NWIN
    phases = 2.0 * math.pi * turns.astype(jnp.float32) / NWIN
    cos_rows = scaling * window[None, :] * jnp.cos(phases)
    sin_rows = -scaling * window[None, :] * jnp.sin(phases)
    return jnp.concatenate([cos_rows, sin_rows], axis=0).astype(jnp.bfloat16)


def on_device(snapshots, starts, bins, mode_count):
    time_dev, all_points = snapshots.shape
    groups = lax.axis_size("space")
    points_dev = all_points // groups
    fourier_table = make_table(bins)
    arranged = snapshots.reshape(time_dev, groups, points_dev)
    series = lax.all_to_all(arranged, "space", split_axis=1, concat_axis=0, tiled=True)[:, 0, :]
    time_mean = jnp.mean(series.astype(jnp.float32), axis=0)
    centered = (series.astype(jnp.float32) - time_mean[None, :]).astype(jnp.bfloat16)

    def take_block(first):
        return lax.dynamic_slice_in_dim(centered, first, NWIN, 0)

    welch_windows = jax.vmap(take_block)(starts)
    matrix_product = jnp.einsum(
        "vx,oxy->voy", fourier_table, welch_windows, preferred_element_type=jnp.float32
    )
    spectra = matrix_product.astype(jnp.bfloat16)
    real_component = spectra[:NFREQ]
    imag_part = spectra[NFREQ:]
    stacked = jnp.concatenate([real_component, imag_part], axis=1)
    local_gram = jnp.einsum("fip,fjp->fij", stacked, stacked, preferred_element_type=jnp.float32)
    gram = lax.psum(local_gram, "space")
    real_real = gram[:, :NB, :NB]
    real_imag = gram[:, :NB, NB:]
    imag_real = gram[:, NB:, :NB]
    imag_imag = gram[:, NB:, NB:]
    summed = real_real + imag_imag
    skew_part = real_imag - imag_real
    upper_rows = jnp.concatenate([summed, -skew_part], axis=2)
    lower_rows = jnp.concatenate([skew_part, summed], axis=2)
    cross = jnp.concatenate([upper_rows, lower_rows], axis=1) / jnp.float32(all_points)
    lower_cholesky_matrix = jnp.linalg.cholesky(cross)
    signed = jnp.concatenate([real_component, -imag_part], axis=1).astype(jnp.float32)

    def solve_one(matrix, values):
        return jax.scipy.linalg.solve_triangular(matrix, values, lower=True)

    basis = jax.vmap(solve_one)(lower_cholesky_matrix, signed)
    row_index = jnp.arange(2 * NB, dtype=jnp.int32) % NB
    keep = row_index[None, :, None] < mode_count[:, None, None]
    modes = jnp.where(keep, basis, jnp.zeros_like(basis)).astype(jnp.bfloat16)
    factor = jnp.swapaxes(lower_cholesky_matrix, 1, 2)
    return (modes, factor)


def solution(mesh):
    in_specs = (P("space", "parts"), P(), P(), P())
    out_specs = (P(None, None, ("parts", "space")), P("parts", None, None))
    return jax.shard_map(
        on_device, mesh=mesh, in_specs=in_specs, out_specs=out_specs, check_vma=False
    )
```

profile of v0, /device:TPU:1, one launch (start us, length us, event | category | flops | bytes accessed | tf_op | source)
XLA Modules:
  0.0 287.9 jit_solution(15959052177133936224)
XLA Ops:
  7.2 2.4 copy.33
  9.5 7.3 %all-to-all-start = ((bf16[136,16,256]{2,0,1:T(8,128)(2,1)}), bf16[136,16,256]{2,0,1:T(8,128)(2,1)S(1)}, u32[]{:S(2)}, u32[]{:S(2)}) async-start(bf16[136,16,256]{2,0,1:T(8,128)(2,1)} %bitcast.30), calls=%async_computation | async-start | bytes 2228224 | tf_op jit(solution)/shard_map/all_to_all | solution.py:29
  16.9 0.6 multiply_reduce_fusion
  18.4 0.1 broadcast_compare_fusion
  18.5 0.2 multiply_convert_fusion.1
  18.7 22.5 %all-to-all-done = bf16[136,16,256]{2,0,1:T(8,128)(2,1)S(1)} async-done(((bf16[136,16,256]{2,0,1:T(8,128)(2,1)}), bf16[136,16,256]{2,0,1:T(8,128)(2,1)S(1)}, u32[]{:S(2)}, u32[]{:S(2)}) %all-to-all-start) | async-done | bytes 1114144 | tf_op jit(solution)/shard_map/all_to_all | solution.py:29
  41.2 0.3 convert_reduce_fusion
  41.5 0.2 fusion
  41.8 30.8 %while.1 = (s32[]{:T(128)}, bf16[2176,256]{1,0:T(8,128)(2,1)S(1)}, s32[16,2]{0,1:T(2,128)S(1)}, bf16[16,256,256]{2,1,0:T(8,128)(2,1)}, s32[]{:T(128)}) while((s32[]{:T(128)}, bf16[2176,256]{1,0:T(8,128)(2,1)S(1)}, s32[16,2]{0,1:T(2,128)S(1)}, bf16[16,256,256]{2,1,0:T(8,128)(2,1)}, s32[]{:T(128)}) %tuple.30), condition=%wide.while_cond, body=%wide.while_body.sunk | while | flops 2 | bytes 262757 | solution.py:34
  41.8 0.1 constant_dynamic-slice_fusion.2
  41.8 0.5 slice.63
  42.4 1.3 bitcast_dynamic-update-slice_fusion.2
  43.7 0.1 constant_dynamic-slice_fusion.2
  43.8 0.5 slice.63
  44.3 1.3 bitcast_dynamic-update-slice_fusion.2
  45.6 0.1 constant_dynamic-slice_fusion.2
  45.7 0.5 slice.63
  46.2 1.3 bitcast_dynamic-update-slice_fusion.2
  47.5 0.1 constant_dynamic-slice_fusion.2
  47.6 0.5 slice.63
  48.1 1.3 bitcast_dynamic-update-slice_fusion.2
  49.5 0.1 constant_dynamic-slice_fusion.2
  49.5 0.5 slice.63
  50.0 1.3 bitcast_dynamic-update-slice_fusion.2
  51.4 0.1 constant_dynamic-slice_fusion.2
  51.4 0.5 slice.63
  52.0 1.3 bitcast_dynamic-update-slice_fusion.2
  53.3 0.1 constant_dynamic-slice_fusion.2
  53.4 0.5 slice.63
  53.9 1.3 bitcast_dynamic-update-slice_fusion.2
  55.3 0.5 slice.63
  55.8 1.3 bitcast_dynamic-update-slice_fusion.2
  57.2 0.5 slice.63
  57.7 1.3 bitcast_dynamic-update-slice_fusion.2
  59.2 0.5 slice.63
  59.7 1.3 bitcast_dynamic-update-slice_fusion.2
  61.1 0.5 slice.63
  61.6 1.3 bitcast_dynamic-update-slice_fusion.2
  63.0 0.5 slice.63
  63.5 1.3 bitcast_dynamic-update-slice_fusion.2
  64.9 0.5 slice.63
  65.5 1.3 bitcast_dynamic-update-slice_fusion.2
  66.9 0.5 slice.63
  67.4 1.3 bitcast_dynamic-update-slice_fusion.2
  68.8 0.5 slice.63
  69.3 1.3 bitcast_dynamic-update-slice_fusion.2
  70.7 0.5 slice.63
  71.2 1.3 bitcast_dynamic-update-slice_fusion.2
  72.6 2.1 convolution_convert_fusion
  74.7 0.1 pad_maximum_fusion
  74.8 1.2 fusion.4
  76.0 92.4 %all-reduce.3.cloned.1.call-done = f32[32,32,32]{1,2,0:T(8,128)} async-done(((f32[32,32,32]{1,2,0:T(8,128)}), f32[32,32,32]{1,2,0:T(8,128)}) %all-reduce.3.cloned.1.call-update) | async-done | bytes 131088 | tf_op jit(solution)/shard_map/psum | solution.py:45
  168.5 1.4 fusion.17
  169.9 0.2 maximum_multiply_fusion
  170.1 0.2 copy.20
  170.3 0.2 fusion.2
  170.5 93.8 %custom-call.8 = f32[32,32,32]{2,1,0:T(8,128)S(1)} custom-call(f32[32,32,32]{2,1,0:T(8,128)S(1)} %fusion.2), custom_call_target="Cholesky" | custom-call | tf_op jit(solution)/shard_map/jit(cholesky)/cholesky | solution.py:55
  264.2 0.3 copy.21
  264.6 0.2 select_reduce_fusion
  264.8 0.2 fusion.6
  265.0 12.5 %custom-call.9 = f32[32,1,32,32]{0,2,3,1:T(8,128)S(1)} custom-call(f32[32,1,32,32]{0,3,2,1:T(8,128)S(1)} %get-tuple-element.25), custom_call_target="InvertDiagBlocksLowerTriangular" | custom-call | tf_op jit(solution)/shard_map/vmap(jit(_solve_triangular))/triangular_solve | solution.py:59
  277.5 0.6 copy.23
  278.1 1.3 copy.25
  279.4 1.6 fusion.1
  (27 shorter events, 0.9 us)
Async XLA Ops:
  7.2 11.1 %copy-start.2 = (s32[16]{0:T(128)S(1)}, s32[16]{0:T(128)}, u32[]{:S(2)}) copy-start(s32[16]{0:T(128)} %param.5) | copy-start | bytes 196
  7.2 11.2 %copy-start.1 = (s32[32]{0:T(128)S(1)}, s32[32]{0:T(128)}, u32[]{:S(2)}) copy-start(s32[32]{0:T(128)} %param.7) | copy-start | bytes 388
  7.2 11.3 %copy-start = (s32[32]{0:T(128)S(1)}, s32[32]{0:T(128)}, u32[]{:S(2)}) copy-start(s32[32]{0:T(128)} %param.6) | copy-start | bytes 388
  9.5 31.7 %all-to-all-start = ((bf16[136,16,256]{2,0,1:T(8,128)(2,1)}), bf16[136,16,256]{2,0,1:T(8,128)(2,1)S(1)}, u32[]{:S(2)}, u32[]{:S(2)}) async-start(bf16[136,16,256]{2,0,1:T(8,128)(2,1)} %bitcast.30), calls=%async_computation | async-start | bytes 2228224 | tf_op jit(solution)/shard_map/all_to_all | solution.py:29
  16.9 151.6 %all-reduce.3.cloned.1.call-start = ((), (), s32[]{:S(2)}) async-start(), calls=%async_computation.1 | async-start | bytes 1048576 | tf_op jit(solution)/shard_map/psum | solution.py:45
Sparse Core Ops, SparseCore 0:
  76.1 92.2 all-reduce.2
where the time goes:
time: 288 us
  waiting for transfers between devices  115 us (40%)
  other arithmetic  110 us (38%)
  local copies, waits for them, and re-layouts  35.5 us (12%)
  between operations  14.9 us (5%)
  starting transfers between devices  7.36 us (3%)
  matrix products  4.92 us (2%)
    another operation x4, other arithmetic, on_device(): lower_cholesky_matrix = jnp.linalg.cholesky(cross)  94 us
    psum x1, waiting for transfers between devices, on_device(): gram = lax.psum(local_gram, 'space')  92.4 us
    gather x48, local copies, waits for them, and re-layouts  30.8 us
    all_to_all x1, waiting for transfers between devices, on_device(): lax.all_to_all(arranged, 'space', split_axis=1, concat_axis=0, tiled=True)  22.5 us
    another operation x2, other arithmetic, solve_one(): return jax.scipy.linalg.solve_triangular(matrix, values, lower=True)  12.5 us
    all_to_all x1, starting transfers between devices, on_device(): lax.all_to_all(arranged, 'space', split_axis=1, concat_axis=0, tiled=True)  7.32 us
  transfers between devices with their start and end apart: 2, of which 2 were waited for; matrix products, arithmetic and copies ran while one was open for 0% of the time, Pallas kernels for 0%

commit v1 on v0

--- a/solution.py
+++ b/solution.py
@@ -26,7 +26,12 @@
     points_dev = all_points // groups
     fourier_table = make_table(bins)
     arranged = snapshots.reshape(time_dev, groups, points_dev)
-    series = lax.all_to_all(arranged, "space", split_axis=1, concat_axis=0, tiled=True)[:, 0, :]
+    series = jnp.concatenate(
+        lax.all_to_all(
+            jnp.stack(jnp.split(arranged, lax.axis_size("space"), axis=1), axis=0), "space", 0, 0
+        ),
+        axis=0,
+    )[:, 0, :]
     time_mean = jnp.mean(series.astype(jnp.float32), axis=0)
     centered = (series.astype(jnp.float32) - time_mean[None, :]).astype(jnp.bfloat16)
 

time: 288 us -> 299 us (1.038)
  local copies, waits for them, and re-layouts: 35.5 us -> 46.5 us
    unnamed x7 -> x23, local copies, waits for them, and re-layouts: 1.33 us -> 12.3 us
where the time goes in v1:
time: 299 us
  waiting for transfers between devices  115 us (38%)
  other arithmetic  110 us (37%)
  local copies, waits for them, and re-layouts  46.5 us (16%)
  between operations  14.9 us (5%)
  starting transfers between devices  7.49 us (3%)
  matrix products  4.92 us (2%)
    another operation x4, other arithmetic, on_device(): lower_cholesky_matrix = jnp.linalg.cholesky(cross)  94 us
    psum x1, waiting for transfers between devices, on_device(): gram = lax.psum(local_gram, 'space')  92.4 us
    gather x48, local copies, waits for them, and re-layouts  30.7 us
    all_to_all x1, waiting for transfers between devices, on_device(): lax.all_to_all(jnp.stack(jnp.split(arranged, lax.axis_size('space'), axis...  22.5 us
    another operation x2, other arithmetic, solve_one(): return jax.scipy.linalg.solve_triangular(matrix, values, lower=True)  12.5 us
    unnamed x23, local copies, waits for them, and re-layouts  12.3 us
    all_to_all x1, starting transfers between devices, on_device(): lax.all_to_all(jnp.stack(jnp.split(arranged, lax.axis_size('space'), axis...  7.45 us
  transfers between devices with their start and end apart: 2, of which 2 were waited for; matrix products, arithmetic and copies ran while one was open for 0% of the time, Pallas kernels for 0%

profile of v1, /device:TPU:1, one launch (start us, length us, event | category | flops | bytes accessed | tf_op | source)
XLA Modules:
  0.0 299.0 jit_solution(11118423231322477086)
XLA Ops:
  7.2 1.5 copy.330
  8.7 1.8 fusion.18
  10.5 0.6 bitcast_dynamic-update-slice_fusion.16
  11.2 0.6 bitcast_dynamic-update-slice_fusion.15
  11.8 0.6 bitcast_dynamic-update-slice_fusion.14
  12.4 0.6 bitcast_dynamic-update-slice_fusion.13
  13.1 0.6 bitcast_dynamic-update-slice_fusion.12
  13.7 0.6 bitcast_dynamic-update-slice_fusion.11
  14.3 0.6 bitcast_dynamic-update-slice_fusion.10
  14.9 0.6 bitcast_dynamic-update-slice_fusion.9
  15.6 0.6 bitcast_dynamic-update-slice_fusion.8
  16.2 0.6 bitcast_dynamic-update-slice_fusion.7
  16.8 0.6 bitcast_dynamic-update-slice_fusion.6
  17.5 0.6 bitcast_dynamic-update-slice_fusion.5
  18.1 0.6 bitcast_dynamic-update-slice_fusion.4
  18.7 0.6 bitcast_dynamic-update-slice_fusion.3
  19.4 0.6 bitcast_dynamic-update-slice_fusion.2
  20.0 0.6 bitcast_dynamic-update-slice_fusion.1
  20.6 7.5 %all-to-all-start = ((bf16[16,136,1,256]{3,1,2,0:T(8,128)(2,1)}), bf16[16,136,1,256]{3,1,2,0:T(8,128)(2,1)S(1)}, u32[]{:S(2)}, u32[]{:S(2)}) async-start(bf16[16,136,1,256]{3,1,2,0:T(8,128)(2,1)} %bitcast_dynamic-update-slice_fusion.1), calls=%async_computation | async-start | bytes 2228224 | tf_op jit(solution)/shard_map/all_to_all | solution.py:30
  28.1 0.6 multiply_reduce_fusion
  29.9 22.5 %all-to-all-done = bf16[16,136,1,256]{3,1,2,0:T(8,128)(2,1)S(1)} async-done(((bf16[16,136,1,256]{3,1,2,0:T(8,128)(2,1)}), bf16[16,136,1,256]{3,1,2,0:T(8,128)(2,1)S(1)}, u32[]{:S(2)}, u32[]{:S(2)}) %all-to-all-start) | async-done | bytes 1114144 | tf_op jit(solution)/shard_map/all_to_all | solution.py:30
  53.0 30.7 %while.1 = (s32[]{:T(128)}, bf16[2176,256]{1,0:T(8,128)(2,1)S(1)}, s32[16,2]{0,1:T(2,128)S(1)}, bf16[16,256,256]{2,1,0:T(8,128)(2,1)}, s32[]{:T(128)}) while((s32[]{:T(128)}, bf16[2176,256]{1,0:T(8,128)(2,1)S(1)}, s32[16,2]{0,1:T(2,128)S(1)}, bf16[16,256,256]{2,1,0:T(8,128)(2,1)}, s32[]{:T(128)}) %tuple.62), condition=%wide.while_cond, body=%wide.while_body.sunk | while | flops 2 | bytes 263257 | solution.py:39
  53.1 0.5 slice.63
  53.6 1.3 bitcast_dynamic-update-slice_fusion.18
  55.0 0.5 slice.63
  55.5 1.3 bitcast_dynamic-update-slice_fusion.18
  56.9 0.5 slice.63
  57.4 1.3 bitcast_dynamic-update-slice_fusion.18
  58.8 0.5 slice.63
  59.3 1.3 bitcast_dynamic-update-slice_fusion.18
  60.7 0.5 slice.63
  61.2 1.3 bitcast_dynamic-update-slice_fusion.18
  62.6 0.5 slice.63
  63.2 1.3 bitcast_dynamic-update-slice_fusion.18
  64.6 0.5 slice.63
  65.1 1.3 bitcast_dynamic-update-slice_fusion.18
  66.5 0.5 slice.63
  67.0 1.3 bitcast_dynamic-update-slice_fusion.18
  68.4 0.5 slice.63
  68.9 1.3 bitcast_dynamic-update-slice_fusion.18
  70.3 0.5 slice.63
  70.8 1.3 bitcast_dynamic-update-slice_fusion.18
  72.2 0.5 slice.63
  72.8 1.3 bitcast_dynamic-update-slice_fusion.18
  74.2 0.5 slice.63
  74.7 1.3 bitcast_dynamic-update-slice_fusion.18
  76.1 0.5 slice.63
  76.6 1.3 bitcast_dynamic-update-slice_fusion.18
  78.0 0.5 slice.63
  78.5 1.3 bitcast_dynamic-update-slice_fusion.18
  79.9 0.5 slice.63
  80.4 1.3 bitcast_dynamic-update-slice_fusion.18
  81.8 0.5 slice.63
  82.4 1.3 bitcast_dynamic-update-slice_fusion.18
  83.7 2.1 convolution_convert_fusion
  85.9 1.2 fusion.4
  87.2 92.4 %all-reduce.3.cloned.1.call-done = f32[32,32,32]{1,2,0:T(8,128)} async-done(((f32[32,32,32]{1,2,0:T(8,128)}), f32[32,32,32]{1,2,0:T(8,128)}) %all-reduce.3.cloned.1.call-update) | async-done | bytes 131088 | tf_op jit(solution)/shard_map/psum | solution.py:50
  179.6 1.4 fusion.17
  181.6 93.8 %custom-call.8 = f32[32,32,32]{2,1,0:T(8,128)S(1)} custom-call(f32[32,32,32]{2,1,0:T(8,128)S(1)} %fusion.2), custom_call_target="Cholesky" | custom-call | tf_op jit(solution)/shard_map/jit(cholesky)/cholesky | solution.py:60
  275.4 0.3 copy.308
  276.2 12.5 %custom-call.9 = f32[32,1,32,32]{0,2,3,1:T(8,128)S(1)} custom-call(f32[32,1,32,32]{0,3,2,1:T(8,128)S(1)} %get-tuple-element.75), custom_call_target="InvertDiagBlocksLowerTriangular" | custom-call | tf_op jit(solution)/shard_map/vmap(jit(_solve_triangular))/triangular_solve | solution.py:64
  288.7 0.6 copy.310
  289.2 1.3 copy.312
  290.5 1.6 fusion.1
  (44 shorter events, 3.3 us)
Async XLA Ops:
  20.6 8.9 %copy-start.2 = (s32[16]{0:T(128)S(1)}, s32[16]{0:T(128)}, u32[]{:S(2)}) copy-start(s32[16]{0:T(128)} %param.5) | copy-start | bytes 196
  20.6 9.0 %copy-start.1 = (s32[32]{0:T(128)S(1)}, s32[32]{0:T(128)}, u32[]{:S(2)}) copy-start(s32[32]{0:T(128)} %param.7) | copy-start | bytes 388
  20.6 9.0 %copy-start = (s32[32]{0:T(128)S(1)}, s32[32]{0:T(128)}, u32[]{:S(2)}) copy-start(s32[32]{0:T(128)} %param.6) | copy-start | bytes 388
  20.6 31.8 %all-to-all-start = ((bf16[16,136,1,256]{3,1,2,0:T(8,128)(2,1)}), bf16[16,136,1,256]{3,1,2,0:T(8,128)(2,1)S(1)}, u32[]{:S(2)}, u32[]{:S(2)}) async-start(bf16[16,136,1,256]{3,1,2,0:T(8,128)(2,1)} %bitcast_dynamic-update-slice_fusion.1), calls=%async_computation | async-start | bytes 2228224 | tf_op jit(solution)/shard_map/all_to_all | solution.py:30
  28.1 151.5 %all-reduce.3.cloned.1.call-start = ((), (), s32[]{:S(2)}) async-start(), calls=%async_computation.1 | async-start | bytes 1048576 | tf_op jit(solution)/shard_map/psum | solution.py:50
Sparse Core Ops, SparseCore 0:
  87.3 92.2 all-reduce.2

commit v2 on v0

--- a/solution.py
+++ b/solution.py
@@ -3,6 +3,7 @@
 import jax.numpy as jnp
 from jax import lax
 from jax.sharding import PartitionSpec as P
+from jax.lax import all_gather
 
 NB = 16
 NWIN = 256
@@ -42,7 +43,11 @@
     imag_part = spectra[NFREQ:]
     stacked = jnp.concatenate([real_component, imag_part], axis=1)
     local_gram = jnp.einsum("fip,fjp->fij", stacked, stacked, preferred_element_type=jnp.float32)
-    gram = lax.psum(local_gram, "space")
+
+    def _load_turns(here_x, shard_axis):
+        return all_gather(here_x, shard_axis).sum(axis=0)
+
+    gram = _load_turns(local_gram, "space")
     real_real = gram[:, :NB, :NB]
     real_imag = gram[:, :NB, NB:]
     imag_real = gram[:, NB:, :NB]

time: 288 us -> 277 us (0.962)
  waiting for transfers between devices: 115 us -> 99.6 us
  other arithmetic: 110 us -> 113 us
    psum x1 -> x0, waiting for transfers between devices: 92.4 us -> none  [on_device(): gram = lax.psum(local_gram, 'space')]
    all_gather x0 -> x1, waiting for transfers between devices: none -> 77 us  [_load_turns(): return all_gather(here_x, shard_axis).sum(axis=0)]
    reduce_sum x0 -> x1, other arithmetic: none -> 4.49 us  [_load_turns(): return all_gather(here_x, shard_axis).sum(axis=0)]
where the time goes in v2:
time: 277 us; the launch traced here: 276 us
  other arithmetic  113 us (41%)
  waiting for transfers between devices  99.6 us (36%)
  local copies, waits for them, and re-layouts  36.1 us (13%)
  between operations  14.9 us (5%)
  starting transfers between devices  7.36 us (3%)
  matrix products  4.91 us (2%)
    another operation x4, other arithmetic, on_device(): lower_cholesky_matrix = jnp.linalg.cholesky(cross)  94 us
    all_gather x1, waiting for transfers between devices, _load_turns(): return all_gather(here_x, shard_axis).sum(axis=0)  77 us
    gather x48, local copies, waits for them, and re-layouts  30.7 us
    all_to_all x1, waiting for transfers between devices, on_device(): lax.all_to_all(arranged, 'space', split_axis=1, concat_axis=0, tiled=True)  22.6 us
    another operation x2, other arithmetic, solve_one(): return jax.scipy.linalg.solve_triangular(matrix, values, lower=True)  12.5 us
    all_to_all x1, starting transfers between devices, on_device(): lax.all_to_all(arranged, 'space', split_axis=1, concat_axis=0, tiled=True)  7.32 us
  transfers between devices with their start and end apart: 2, of which 2 were waited for; matrix products, arithmetic and copies ran while one was open for 0% of the time, Pallas kernels for 0%

profile of v2, /device:TPU:1, one launch (start us, length us, event | category | flops | bytes accessed | tf_op | source)
XLA Modules:
  0.0 276.3 jit_solution(13360002624750411451)
XLA Ops:
  7.2 2.3 copy.38
  9.5 7.3 %all-to-all-start = ((bf16[136,16,256]{2,0,1:T(8,128)(2,1)}), bf16[136,16,256]{2,0,1:T(8,128)(2,1)S(1)}, u32[]{:S(2)}, u32[]{:S(2)}) async-start(bf16[136,16,256]{2,0,1:T(8,128)(2,1)} %bitcast.31), calls=%async_computation | async-start | bytes 2228224 | tf_op jit(solution)/shard_map/all_to_all | solution.py:30
  16.9 0.6 multiply_reduce_fusion
  18.3 0.2 multiply_convert_fusion.1
  18.5 22.6 %all-to-all-done = bf16[136,16,256]{2,0,1:T(8,128)(2,1)S(1)} async-done(((bf16[136,16,256]{2,0,1:T(8,128)(2,1)}), bf16[136,16,256]{2,0,1:T(8,128)(2,1)S(1)}, u32[]{:S(2)}, u32[]{:S(2)}) %all-to-all-start) | async-done | bytes 1114144 | tf_op jit(solution)/shard_map/all_to_all | solution.py:30
  41.2 0.3 convert_reduce_fusion
  41.5 0.2 fusion
  41.7 30.7 %while.1 = (s32[]{:T(128)}, bf16[2176,256]{1,0:T(8,128)(2,1)S(1)}, s32[16,2]{0,1:T(2,128)S(1)}, bf16[16,256,256]{2,1,0:T(8,128)(2,1)}, s32[]{:T(128)}) while((s32[]{:T(128)}, bf16[2176,256]{1,0:T(8,128)(2,1)S(1)}, s32[16,2]{0,1:T(2,128)S(1)}, bf16[16,256,256]{2,1,0:T(8,128)(2,1)}, s32[]{:T(128)}) %tuple.32), condition=%wide.while_cond, body=%wide.while_body.sunk | while | flops 2 | bytes 263257 | solution.py:35
  41.7 0.1 constant_dynamic-slice_fusion.2
  41.8 0.5 slice.61
  42.3 1.3 bitcast_dynamic-update-slice_fusion.2
  43.7 0.1 constant_dynamic-slice_fusion.2
  43.7 0.5 slice.61
  44.2 1.3 bitcast_dynamic-update-slice_fusion.2
  45.6 0.5 slice.61
  46.2 1.3 bitcast_dynamic-update-slice_fusion.2
  47.6 0.5 slice.61
  48.1 1.3 bitcast_dynamic-update-slice_fusion.2
  49.5 0.5 slice.61
  50.0 1.3 bitcast_dynamic-update-slice_fusion.2
  51.4 0.5 slice.61
  51.9 1.3 bitcast_dynamic-update-slice_fusion.2
  53.3 0.5 slice.61
  53.8 1.3 bitcast_dynamic-update-slice_fusion.2
  55.2 0.5 slice.61
  55.7 1.3 bitcast_dynamic-update-slice_fusion.2
  57.1 0.5 slice.61
  57.7 1.3 bitcast_dynamic-update-slice_fusion.2
  59.1 0.5 slice.61
  59.6 1.3 bitcast_dynamic-update-slice_fusion.2
  61.0 0.5 slice.61
  61.5 1.3 bitcast_dynamic-update-slice_fusion.2
  62.9 0.5 slice.61
  63.4 1.3 bitcast_dynamic-update-slice_fusion.2
  64.8 0.5 slice.61
  65.3 1.3 bitcast_dynamic-update-slice_fusion.2
  66.8 0.5 slice.61
  67.3 1.3 bitcast_dynamic-update-slice_fusion.2
  68.7 0.5 slice.61
  69.2 1.3 bitcast_dynamic-update-slice_fusion.2
  70.6 0.5 slice.61
  71.1 1.3 bitcast_dynamic-update-slice_fusion.2
  72.4 2.1 convolution_convert_fusion
  74.6 0.1 pad_maximum_fusion
  74.7 1.2 fusion.4
  76.0 0.1 broadcast_compare_fusion
  76.0 77.0 %all-gather.3.cloned.1.call-done = f32[512,32,32]{2,1,0:T(8,128)} async-done(((f32[32,32,32]{2,1,0:T(8,128)}), f32[512,32,32]{2,1,0:T(8,128)}) %all-gather.3.cloned.1.call-update) | async-done | bytes 2097168 | tf_op jit(solution)/shard_map/all_gather | solution.py:48
  153.0 4.5 %reduce_sum.29 = f32[32,32,32]{2,1,0:T(8,128)S(1)} reduce(f32[16,32,32,32]{3,2,1,0:T(8,128)} %bitcast.36, f32[]{:T(128)} %constant.92.clone.1), dimensions={0}, to_apply=%region_2.3 | reduce | flops 491520 | bytes 2228228 | tf_op jit(solution)/shard_map/reduce_sum | solution.py:48
  157.5 0.2 fusion.18
  157.7 0.1 copy.30
  157.8 0.1 copy.31
  158.0 0.1 copy.28
  158.1 0.1 copy.29
  158.3 0.2 maximum_multiply_fusion
  158.5 0.2 copy.22
  158.7 0.2 fusion.2
  159.0 93.8 %custom-call.8 = f32[32,32,32]{2,1,0:T(8,128)S(1)} custom-call(f32[32,32,32]{2,1,0:T(8,128)S(1)} %fusion.2), custom_call_target="Cholesky" | custom-call | tf_op jit(solution)/shard_map/jit(cholesky)/cholesky | solution.py:60
  252.7 0.3 copy.23
  253.0 0.2 select_reduce_fusion
  253.3 0.2 fusion.6
  253.5 12.5 %custom-call.9 = f32[32,1,32,32]{0,2,3,1:T(8,128)S(1)} custom-call(f32[32,1,32,32]{0,3,2,1:T(8,128)S(1)} %get-tuple-element.25), custom_call_target="InvertDiagBlocksLowerTriangular" | custom-call | tf_op jit(solution)/shard_map/vmap(jit(_solve_triangular))/triangular_solve | solution.py:64
  266.0 0.6 copy.25
  266.5 1.3 copy.27
  267.9 1.6 fusion.1
  (34 shorter events, 1.3 us)
Async XLA Ops:
  7.2 11.1 %copy-start.2 = (s32[16]{0:T(128)S(1)}, s32[16]{0:T(128)}, u32[]{:S(2)}) copy-start(s32[16]{0:T(128)} %param.5) | copy-start | bytes 196
  7.2 11.2 %copy-start = (s32[32]{0:T(128)S(1)}, s32[32]{0:T(128)}, u32[]{:S(2)}) copy-start(s32[32]{0:T(128)} %param.6) | copy-start | bytes 388
  9.5 31.7 %all-to-all-start = ((bf16[136,16,256]{2,0,1:T(8,128)(2,1)}), bf16[136,16,256]{2,0,1:T(8,128)(2,1)S(1)}, u32[]{:S(2)}, u32[]{:S(2)}) async-start(bf16[136,16,256]{2,0,1:T(8,128)(2,1)} %bitcast.31), calls=%async_computation | async-start | bytes 2228224 | tf_op jit(solution)/shard_map/all_to_all | solution.py:30
  16.8 136.2 %all-gather.3.cloned.1.call-start = ((), (), s32[]{:S(2)}) async-start(), calls=%async_computation.1 | async-start | bytes 8912896 | tf_op jit(solution)/shard_map/all_gather | solution.py:48
  74.5 1.4 copy-start.1
Sparse Core Ops, SparseCore 0:
  76.0 76.9 all-gather.2
